TPU v7x, 128 devices: a whole 4x4x4 slice. The times are simulated.
128 devices in a mesh: dp: 4 (over x_lo, core), expert: 32 (over y, x_hi, z).
Axes of the slice: x: 4 (x_hi: 2, x_lo: 2; x = x_hi * 2 + x_lo), y: 4, z: 4, core: 2. Of those that a mesh axis runs over, the one named last changes fastest.
Arguments:
- hidden_in: bfloat16 [16384, 2048], P(('dp', 'expert')), may hold values from -6 to 6
- attn_gain: float32 [2048], replicated, may hold values from 0.1 to 1.9
- query_key_value_weight: bfloat16 [2048, 2560], P('expert'), may hold values from -0.125 to 0.125
- q_gain: float32 [128], replicated, may hold values from 0.1 to 1.9
- key_norm_gain: float32 [128], replicated, may hold values from 0.1 to 1.9
- w_out: bfloat16 [2048, 2048], P('expert'), may hold values from -0.125 to 0.125
- moe_gain: float32 [2048], replicated, may hold values from 0.1 to 1.9
- w_gate_up: bfloat16 [128, 2048, 1536], P(('dp', 'expert')), may hold values from -0.125 to 0.125
- w_down: bfloat16 [128, 768, 2048], P(('dp', 'expert')), may hold values from -0.21875 to 0.21875
- kv_pool: bfloat16 [32, 2, 128, 2, 128], P('dp'), may hold values from -160 to 160
- page_table: int32 [32], replicated, may hold values from 0 to 31, each once
- suffix_lengths: int32 [4, 4], replicated, may hold values from 1 to 2560, 4096 in all within a row
- request_group: int32 [4, 4], replicated, may hold values from 0 to 1
- expert_ids: int32 [16384, 8], P(('dp', 'expert')), may hold values from 0 to 127, all different within a row; in each aligned block of 128 rows (0 to 127, 128 to 255, ...) at most 12 rows name the same one
- gate_weights: float32 [16384, 8], P(('dp', 'expert')), may hold values from 0.05 to 0.3
Outputs:
- hidden_out: bfloat16 [16384, 2048], P(('dp', 'expert'))
- suffix_cache: bfloat16 [16384, 512], P(('dp', 'expert'))
Inputs may be any that keep to these rules, and one draw needn't show every extreme that they name: page_table holds each pool page once. `suffix_lengths`: each row sums to 4096; the largest of each row is exactly 2560. `expert_ids`: a token's 8 experts differ; among the 128 rows of one device no expert is named more than 12 times, and that many times in some device.
All inputs are finite; a program needn't handle non-finite values.
Results may differ from a plain program's by a relative error of at most 0.01.
The roundings to bfloat16 on the way count: a program that leaves them out, or rounds other values in their place, can miss the bound.
Values may be sent and summed in bfloat16 or wider, within the bound.
A program may use at most 256 MiB of HBM per device.

v0:
```python
import math
import jax
import jax.numpy as jnp
from jax import lax
from jax.sharding import PartitionSpec as P

PREFIX_TOKENS = 2048
PAGE_TOKENS = 128
eps = 1e-06
theta = 1000000.0
floor_value = -1e30


def root_mean_scale(value_rows, gain):
    value_rows = value_rows.astype(jnp.float32)
    return (
        value_rows
        * lax.rsqrt(jnp.mean(value_rows * value_rows, axis=-1, keepdims=True) + eps)
        * gain
    )


def rotary_apply(value_rows, token_positions):
    half = value_rows.shape[-1] // 2
    freqs = theta ** (-jnp.arange(half, dtype=jnp.float32) / half)
    angles = token_positions.astype(jnp.float32)[:, None] * freqs[None, :]
    cosine = jnp.cos(angles)[:, None, :]
    sine = jnp.sin(angles)[:, None, :]
    first = value_rows[..., :half]
    second_split = value_rows[..., half:]
    return jnp.concatenate(
        [first * cosine - second_split * sine, second_split * cosine + first * sine], axis=-1
    )


def layout(lengths_row, index):
    ends = jnp.cumsum(lengths_row)
    starts = ends - lengths_row
    request = jnp.sum((index[:, None] >= ends[None, :]).astype(jnp.int32), axis=1)
    chosen = request[:, None] == jnp.arange(lengths_row.shape[0], dtype=jnp.int32)[None, :]
    offset = index - jnp.sum(jnp.where(chosen, starts[None, :], 0), axis=1)
    return (request, offset, chosen)


def attend(carry, queries, key_rows, value_rows, mask, scale):
    high, total, acc = carry
    scores = (
        jnp.einsum("qkgd,skd->kgqs", queries, key_rows, preferred_element_type=jnp.float32) * scale
    )
    scores = jnp.where(mask[None, None], scores, -jnp.inf)
    new_high = jnp.maximum(high, jnp.max(scores, axis=-1))
    weights = jnp.exp(scores - new_high[..., None])
    scale_factor = jnp.exp(high - new_high)
    total = total * scale_factor + jnp.sum(weights, axis=-1)
    acc = acc * scale_factor[..., None] + jnp.einsum(
        "kgqs,skd->kgqd",
        weights.astype(jnp.bfloat16),
        value_rows,
        preferred_element_type=jnp.float32,
    )
    return (new_high, total, acc)


def expert_rows(rows, gate_up, down):
    both = jnp.dot(rows, gate_up, preferred_element_type=jnp.float32)
    half = both.shape[1] // 2
    act = (jax.nn.silu(both[:, :half]) * both[:, half:]).astype(jnp.bfloat16)
    return jnp.dot(act, down, preferred_element_type=jnp.float32).astype(jnp.bfloat16)


def local(
    hidden_in,
    attn_gain,
    query_key_value_weight,
    q_gain,
    key_norm_gain,
    w_out,
    moe_gain,
    w_gate_up,
    w_down,
    kv_pool,
    page_table,
    suffix_lengths,
    request_group,
    expert_ids,
    gate_weights,
):
    tokens_here, width = hidden_in.shape
    page_rows = kv_pool.shape[2]
    kv_heads = kv_pool.shape[3]
    head_dim = kv_pool.shape[4]
    key_value_width = kv_heads * head_dim
    query_width = query_key_value_weight.shape[1] - 2 * key_value_width
    q_heads = query_width // head_dim
    head_split = q_heads // kv_heads
    scale = 1.0 / math.sqrt(head_dim)
    row_count = lax.axis_size("dp")
    col_count = lax.axis_size("expert")
    row = lax.axis_index("dp")
    col = lax.axis_index("expert")
    normed = root_mean_scale(hidden_in, attn_gain).astype(jnp.bfloat16)
    part = normed
    qkv = jnp.dot(
        part,
        lax.all_gather(query_key_value_weight, "expert", axis=0, tiled=True),
        preferred_element_type=jnp.float32,
    )
    index = col * tokens_here + jnp.arange(tokens_here, dtype=jnp.int32)
    lengths_row = lax.dynamic_index_in_dim(suffix_lengths, row, 0, keepdims=False)
    groups_row = lax.dynamic_index_in_dim(request_group, row, 0, keepdims=False)
    request, offset, chosen = layout(lengths_row, index)
    qgroup = jnp.sum(jnp.where(chosen, groups_row[None, :], 0), axis=1)
    token_positions = PREFIX_TOKENS + offset
    queries = rotary_apply(
        root_mean_scale(qkv[:, :query_width].reshape(tokens_here, q_heads, head_dim), q_gain),
        token_positions,
    ).astype(jnp.bfloat16)
    key_rows = rotary_apply(
        root_mean_scale(
            qkv[:, query_width : query_width + key_value_width].reshape(
                tokens_here, kv_heads, head_dim
            ),
            key_norm_gain,
        ),
        token_positions,
    ).astype(jnp.bfloat16)
    value_rows = (
        qkv[:, query_width + key_value_width :]
        .reshape(tokens_here, kv_heads, head_dim)
        .astype(jnp.bfloat16)
    )
    suffix_cache = jnp.concatenate(
        [
            key_rows.reshape(tokens_here, key_value_width),
            value_rows.reshape(tokens_here, key_value_width),
        ],
        axis=1,
    )
    grouped = queries.reshape(tokens_here, kv_heads, head_split, head_dim)
    carry = (
        jnp.full((kv_heads, head_split, tokens_here), floor_value, jnp.float32),
        jnp.zeros((kv_heads, head_split, tokens_here), jnp.float32),
        jnp.zeros((kv_heads, head_split, tokens_here, head_dim), jnp.float32),
    )
    piece_keys = lax.all_gather(key_rows, "expert", axis=0, tiled=True)
    piece_values = lax.all_gather(value_rows, "expert", axis=0, tiled=True)
    key_index = jnp.arange(piece_keys.shape[0], dtype=jnp.int32)
    key_request, _, _ = layout(lengths_row, key_index)
    mask = (key_request[None, :] == request[:, None]) & (key_index[None, :] <= index[:, None])
    carry = attend(carry, grouped, piece_keys, piece_values, mask, scale)
    per_group = PREFIX_TOKENS // PAGE_TOKENS
    slot_ids = jnp.arange(page_table.shape[0], dtype=jnp.int32)
    piece = lax.all_gather(kv_pool, "dp", axis=0, tiled=True)
    count = piece.shape[0]
    hit = page_table[None, :] == jnp.arange(count, dtype=jnp.int32)[:, None]
    key_group = jnp.repeat(
        jnp.sum(jnp.where(hit, slot_ids[None, :] // per_group, 0), axis=1), page_rows
    )
    mask = key_group[None, :] == qgroup[:, None]
    carry = attend(
        carry,
        grouped,
        piece[:, 0].reshape(count * page_rows, kv_heads, head_dim),
        piece[:, 1].reshape(count * page_rows, kv_heads, head_dim),
        mask,
        scale,
    )
    mixed = (
        (carry[2] / carry[1][..., None])
        .transpose(2, 0, 1, 3)
        .reshape(tokens_here, query_width)
        .astype(jnp.bfloat16)
    )
    part = mixed
    projected = jnp.dot(
        part,
        lax.all_gather(w_out, "expert", axis=0, tiled=True),
        preferred_element_type=jnp.float32,
    )
    mid = (hidden_in.astype(jnp.float32) + projected).astype(jnp.bfloat16)
    moe_in = root_mean_scale(mid, moe_gain).astype(jnp.bfloat16)
    top_k = expert_ids.shape[1]
    expert_count = row_count * col_count
    capacity = max(2, tokens_here * top_k * 3 // (2 * expert_count))
    flat = expert_ids.reshape(-1)
    onehot = (flat[:, None] == jnp.arange(expert_count, dtype=jnp.int32)[None, :]).astype(jnp.int32)
    slot = jnp.sum((jnp.cumsum(onehot, axis=0) - onehot) * onehot, axis=1)
    place = flat * capacity + slot
    sources = jnp.repeat(moe_in, top_k, axis=0)
    outgoing = jnp.zeros((expert_count * capacity, width), jnp.bfloat16).at[place].set(sources)
    gate_up = w_gate_up[0]
    down = w_down[0]
    received = lax.all_to_all(
        outgoing.reshape(expert_count, capacity, width),
        ("dp", "expert"),
        split_axis=0,
        concat_axis=0,
        tiled=True,
    )
    results = expert_rows(received.reshape(-1, width), gate_up, down).reshape(received.shape)
    returned = lax.all_to_all(results, ("dp", "expert"), split_axis=0, concat_axis=0, tiled=True)
    picked = returned.reshape(expert_count * capacity, width)[place].astype(jnp.float32)
    moe = jnp.sum(picked.reshape(tokens_here, top_k, width) * gate_weights[:, :, None], axis=1)
    hidden_out = (mid.astype(jnp.float32) + moe).astype(jnp.bfloat16)
    return (hidden_out, suffix_cache)


def solution(mesh):
    return jax.shard_map(
        local,
        mesh=mesh,
        in_specs=(
            P(("dp", "expert"), None),
            P(),
            P("expert", None),
            P(),
            P(),
            P("expert", None),
            P(),
            P(("dp", "expert"), None, None),
            P(("dp", "expert"), None, None),
            P("dp", None, None, None, None),
            P(),
            P(),
            P(),
            P(("dp", "expert"), None),
            P(("dp", "expert"), None),
        ),
        out_specs=(P(("dp", "expert"), None), P(("dp", "expert"), None)),
        check_vma=False,
    )
```

profile of v0, /device:TPU:67, one launch (start us, length us, event | category | flops | bytes accessed | tf_op | source)
XLA Modules:
  0.0 756.2 jit_solution(2184994517330569896)
XLA Ops:
  14.0 114.5 %all-gather.6.cloned.1.call-done = bf16[2048,2560]{1,0:T(8,128)(2,1)} async-done(((bf16[64,2560]{1,0:T(8,128)(2,1)}), bf16[2048,2560]{1,0:T(8,128)(2,1)}) %all-gather.6.cloned.1.call-update) | async-done | bytes 10485776 | tf_op jit(solution)/shard_map/all_gather | solution.py:105
  128.5 5.7 fusion.68
  154.3 21.2 %all-gather.12.cloned.1.call-done = bf16[32,2,128,2,128]{4,2,3,1,0:T(8,128)(2,1)} async-done(((bf16[8,2,128,2,128]{4,2,3,1,0:T(8,128)(2,1)}), bf16[32,2,128,2,128]{4,2,3,1,0:T(8,128)(2,1)}) %all-gather.12.cloned.1.call-update) | async-done | bytes 4194320 | tf_op jit(solution)/shard_map/all_gather | solution.py:153
  196.5 13.6 %bitcast_reduce_fusion = (f32[2,8,128]{2,1,0:T(8,128)S(1)}, f32[2,128,8,4096]{3,1,2,0:T(8,128)}) fusion(pred[128,4096]{1,0:T(8,128)(4,1)S(1)} %copy-done.2, bf16[4096,2,128,1]{2,0,3,1:T(8,128)(2,1)S(1)} %bitcast.168, bf16[128,2,8,64]{3,0,2,1:T(8,128)(2,1)S(1)} %bitcast.171, bf16[128,2,8,64]{3,0,2,1:T(8,128)(2,1)S(1)} %bitcast.169), kind=kOutput, calls=%fused_computation.3 | convolution fusion | flops 2173696000 | bytes 36708352 | tf_op jit(solution)/shard_map/qkgd,skd->kgqs/dot_general | solution.py:48
  210.1 38.8 %all-gather.8.cloned.1.call-done = bf16[4096,2,128]{2,0,1:T(8,128)(2,1)} async-done(((bf16[128,2,128]{2,0,1:T(8,128)(2,1)}), bf16[4096,2,128]{2,0,1:T(8,128)(2,1)}) %all-gather.8.cloned.1.call-update) | async-done | bytes 2097168 | tf_op jit(solution)/shard_map/all_gather | solution.py:145
  249.0 15.0 %fusion.3 = (f32[2,8,128]{2,1,0:T(8,128)S(1)}, f32[2,4096,128,8]{2,1,3,0:T(8,128)}) fusion(pred[128,4096]{0,1:T(8,128)(4,1)} %fusion.29, bf16[128,2,8,64]{3,0,2,1:T(8,128)(2,1)} %bitcast.172, bf16[128,2,8,64]{3,0,2,1:T(8,128)(2,1)} %bitcast.170, bf16[4096,2,128]{2,0,1:T(8,128)(2,1)} %all-gather.8.cloned.1.call-done), kind=kOutput, calls=%fused_computation.10 | convolution fusion | flops 2173696000 | bytes 36708352 | tf_op jit(solution)/shard_map/qkgd,skd->kgqs/dot_general | solution.py:48
  264.0 16.4 %fusion.1 = f32[2,8,128]{2,1,0:T(8,128)S(1)} fusion(f32[2,4096,128,8]{2,1,3,0:T(8,128)} %get-tuple-element.22, f32[2,8,128]{2,1,0:T(8,128)S(1)} %get-tuple-element.16, pred[128,4096]{0,1:T(8,128)(4,1)S(1)} %copy-done.4), kind=kLoop, calls=%fused_computation.8 | loop fusion | flops 33552384 | bytes 34095104 | tf_op jit(solution)/shard_map/reduce_sum | solution.py:54
  284.2 9.5 %fusion.4 = f32[2,8,128]{2,1,0:T(8,128)S(1)} fusion(f32[2,128,8,4096]{3,1,2,0:T(8,128)S(1)} %copy-done.1, f32[2,8,128]{2,1,0:T(8,128)S(1)} %get-tuple-element.15, pred[128,4096]{1,0:T(8,128)(4,1)S(1)} %copy-done.3), kind=kLoop, calls=%fused_computation.11 | loop fusion | flops 33552384 | bytes 34095104 | tf_op jit(solution)/shard_map/reduce_sum | solution.py:54
  293.8 28.9 %all-gather.10.cloned.1.call-done = bf16[4096,2,128]{0,2,1:T(8,128)(2,1)} async-done(((bf16[128,2,128]{0,2,1:T(8,128)(2,1)}), bf16[4096,2,128]{0,2,1:T(8,128)(2,1)}) %all-gather.10.cloned.1.call-update) | async-done | bytes 2097168 | tf_op jit(solution)/shard_map/all_gather | solution.py:146
  322.7 16.3 %fusion.50 = f32[128,2,8,128]{0,3,2,1:T(8,128)} fusion(f32[2,4096,128,8]{2,1,3,0:T(8,128)} %get-tuple-element.22, f32[2,8,128]{2,1,0:T(8,128)S(1)} %get-tuple-element.16, pred[128,4096]{0,1:T(8,128)(4,1)} %fusion.29, bf16[4096,2,128]{0,2,1:T(8,128)(2,1)} %all-gather.10.cloned.1.call-done, f32[128,2,8]{0,2,1:T(8,128)S(1)} %get-tuple-element.5, ...), kind=kOutput, calls=%fused_computation.45 | convolution fusion | flops 2181562368 | bytes 37249024 | tf_op jit(solution)/shard_map/kgqs,skd->kgqd/dot_general | solution.py:55
  339.0 16.3 %fusion.60 = bf16[128,2,8,128]{0,3,2,1:T(8,128)(2,1)} fusion(f32[128,2,8,128]{0,3,2,1:T(8,128)} %fusion.50, bf16[4096,2,128,1]{0,2,1,3:T(8,128)(2,1)} %reshape.374, f32[2,128,8,4096]{3,1,2,0:T(8,128)} %get-tuple-element.20, f32[2,8,128]{2,1,0:T(8,128)S(1)} %get-tuple-element.15, pred[128,4096]{1,0:T(8,128)(4,1)} %broadcast_compare_fusion, ...), kind=kOutput, calls=%fused_computation.47 | convolution fusion | flops 2181824512 | bytes 37765120 | tf_op jit(solution)/shard_map/kgqs,skd->kgqd/dot_general | solution.py:55
  355.4 73.6 %all-gather.14.cloned.1.call-done = bf16[2048,2048]{1,0:T(8,128)(2,1)} async-done(((bf16[64,2048]{1,0:T(8,128)(2,1)}), bf16[2048,2048]{1,0:T(8,128)(2,1)}) %all-gather.14.cloned.1.call-update) | async-done | bytes 8388624 | tf_op jit(solution)/shard_map/all_gather | solution.py:177
  435.9 10.9 %scatter_custom_fusion = bf16[1536,2048]{1,0:T(8,128)(2,1)} fusion(s32[1024]{0:T(1024)S(1)} %bitcast.176, bf16[]{:T(256)} %constant.80.clone.1, bf16[128,2048]{1,0:T(8,128)(2,1)} %multiply_convert_fusion), kind=kCustom, calls=%fused_computation.24 | custom fusion | bytes 6815746 | tf_op jit(solution)/shard_map/scatter | solution.py:190
  446.8 10.6 %reshape.350 = bf16[128,12,2048]{2,1,0:T(8,128)(2,1)} reshape(bf16[1536,2048]{1,0:T(8,128)(2,1)} %scatter_custom_fusion) | data formatting | bytes 12582912 | tf_op jit(solution)/shard_map/reshape | solution.py:194
  457.4 105.0 %all_to_all.10 = bf16[128,12,2048]{2,1,0:T(8,128)(2,1)} all-to-all(bf16[128,12,2048]{2,1,0:T(8,128)(2,1)} %reshape.350), channel_id=1, replica_groups=mesh['dp'=4,'expert'=32] {'dp','expert'}, dimensions={0} | all-to-all | bytes 12582912 | tf_op jit(solution)/shard_map/all_to_all | solution.py:193
  562.4 10.7 %reshape.351 = bf16[1536,2048]{1,0:T(8,128)(2,1)} reshape(bf16[128,12,2048]{2,1,0:T(8,128)(2,1)} %all_to_all.10) | data formatting | bytes 12582912 | tf_op jit(solution)/shard_map/reshape | solution.py:200
  573.1 14.1 %fusion.13 = f32[1536,1536]{1,0:T(8,128)S(1)} fusion(bf16[1536,2048]{1,0:T(8,128)(2,1)} %reshape.351, bf16[1,2048,1536]{2,1,0:T(8,128)(2,1)} %param.22), kind=kOutput, calls=%fused_computation.20 | convolution fusion | flops 9663676416 | bytes 22020096 | tf_op jit(solution)/shard_map/dot_general | solution.py:65
  587.3 7.1 convolution_convert_fusion
  594.3 10.6 %reshape.352 = bf16[128,12,2048]{2,1,0:T(8,128)(2,1)} reshape(bf16[1536,2048]{1,0:T(8,128)(2,1)} %convolution_convert_fusion) | data formatting | bytes 12582912 | tf_op jit(solution)/shard_map/reshape | solution.py:200
  604.9 7.6 %all-to-all-start.1 = ((bf16[128,12,2048]{2,1,0:T(8,128)(2,1)}), bf16[128,12,2048]{2,1,0:T(8,128)(2,1)}, u32[]{:S(2)}, u32[]{:S(2)}) async-start(bf16[128,12,2048]{2,1,0:T(8,128)(2,1)} %reshape.352), calls=%async_computation.1 | async-start | bytes 16777216 | tf_op jit(solution)/shard_map/all_to_all | solution.py:201
  613.5 104.1 %all-to-all-done.1 = bf16[128,12,2048]{2,1,0:T(8,128)(2,1)} async-done(((bf16[128,12,2048]{2,1,0:T(8,128)(2,1)}), bf16[128,12,2048]{2,1,0:T(8,128)(2,1)}, u32[]{:S(2)}, u32[]{:S(2)}) %all-to-all-start.1) | async-done | bytes 6291488 | tf_op jit(solution)/shard_map/all_to_all | solution.py:201
  717.5 10.7 %reshape.353 = bf16[1536,2048]{1,0:T(8,128)(2,1)} reshape(bf16[128,12,2048]{2,1,0:T(8,128)(2,1)} %all-to-all-done.1) | data formatting | bytes 12582912 | tf_op jit(solution)/shard_map/reshape | solution.py:202
  728.2 12.4 %gather_fusion = bf16[1024,2048]{1,0:T(8,128)(2,1)} fusion(bf16[1536,2048]{1,0:T(8,128)(2,1)} %reshape.353, s32[1024]{0:T(1024)S(1)} %broadcast_clamp_fusion), kind=kCustom, calls=%fused_computation | custom fusion | bytes 8392704 | tf_op jit(solution)/shard_map/gather | solution.py:202
  740.7 6.5 fusion.12
  (125 shorter events, 61.4 us)
Async XLA Ops:
  7.2 580.1 %copy-start = (bf16[1,768,2048]{2,1,0:T(8,128)(2,1)S(1)}, bf16[1,768,2048]{2,1,0:T(8,128)(2,1)}, u32[]{:S(2)}) copy-start(bf16[1,768,2048]{2,1,0:T(8,128)(2,1)} %param.23) | copy-start | bytes 9437188
  7.2 121.3 %all-gather.6.cloned.1.call-start = ((), (), s32[]{:S(2)}) async-start(), calls=%async_computation.2 | async-start | bytes 10813440 | tf_op jit(solution)/shard_map/all_gather | solution.py:105
  7.9 167.6 %all-gather.12.cloned.1.call-start = ((), (), s32[]{:S(2)}) async-start(), calls=%async_computation.5 | async-start | bytes 5242880 | tf_op jit(solution)/shard_map/all_gather | solution.py:153
  10.6 238.4 %all-gather.8.cloned.1.call-start = ((), (), s32[]{:S(2)}) async-start(), calls=%async_computation.3 | async-start | bytes 2162688 | tf_op jit(solution)/shard_map/all_gather | solution.py:145
  14.0 124.9 %copy-start.21 = (f32[128]{0:T(128)S(1)}, f32[128]{0:T(128)}, u32[]{:S(2)}) copy-start(f32[128]{0:T(128)} %param.19) | copy-start | bytes 1540
  14.0 129.0 %copy-start.18 = (s32[128,8]{0,1:T(8,128)S(1)}, s32[128,8]{0,1:T(8,128)}, u32[]{:S(2)}) copy-start(s32[128,8]{0,1:T(8,128)} %param.28) | copy-start | bytes 12292
  14.0 132.2 %copy-start.23 = (s32[32]{0:T(128)S(1)}, s32[32]{0:T(128)}, u32[]{:S(2)}) copy-start(s32[32]{0:T(128)} %param.25) | copy-start | bytes 388
  134.3 1.1 copy-start.8
  140.5 182.2 %all-gather.10.cloned.1.call-start = ((), (), s32[]{:S(2)}) async-start(), calls=%async_computation.4 | async-start | bytes 2162688 | tf_op jit(solution)/shard_map/all_gather | solution.py:146
  141.5 1.4 copy-start.16
  142.2 286.7 %all-gather.14.cloned.1.call-start = ((), (), s32[]{:S(2)}) async-start(), calls=%async_computation.6 | async-start | bytes 8650752 | tf_op jit(solution)/shard_map/all_gather | solution.py:177
  179.5 13.5 %copy-start.22 = (f32[128]{0:T(128)S(1)}, f32[128]{0:T(128)}, u32[]{:S(2)}) copy-start(f32[128]{0:T(128)} %param.18) | copy-start | bytes 1540
  193.0 3.4 copy-start.2
  193.1 3.4 copy-start.7
  249.0 15.0 %copy-start.4 = (pred[128,4096]{0,1:T(8,128)(4,1)S(1)}, pred[128,4096]{0,1:T(8,128)(4,1)}, u32[]{:S(2)}) copy-start(pred[128,4096]{0,1:T(8,128)(4,1)} %fusion.29) | copy-start | bytes 1572868
  263.9 20.3 %copy-start.1 = (f32[2,128,8,4096]{3,1,2,0:T(8,128)S(1)}, f32[2,128,8,4096]{3,1,2,0:T(8,128)}, u32[]{:S(2)}) copy-start(f32[2,128,8,4096]{3,1,2,0:T(8,128)} %get-tuple-element.20) | copy-start | bytes 100663296
  264.0 20.3 %copy-start.3 = (pred[128,4096]{1,0:T(8,128)(4,1)S(1)}, pred[128,4096]{1,0:T(8,128)(4,1)}, u32[]{:S(2)}) copy-start(pred[128,4096]{1,0:T(8,128)(4,1)} %broadcast_compare_fusion) | copy-start | bytes 1572868
  429.0 6.0 copy-start.19
  433.9 1.0 copy-start.5
  604.9 7.7 %copy-start.20 = (f32[128,8]{0,1:T(8,128)S(1)}, f32[128,8]{0,1:T(8,128)}, u32[]{:S(2)}) copy-start(f32[128,8]{0,1:T(8,128)} %param.29) | copy-start | bytes 12292
  604.9 7.8 %copy-start.13 = (bf16[128,2,64]{2,0,1:T(8,128)(2,1)S(1)}, bf16[128,2,64]{2,0,1:T(8,128)(2,1)}, u32[]{:S(2)}) copy-start(bf16[128,2,64]{2,0,1:T(8,128)(2,1)} %copy-done.12) | copy-start | bytes 98308
  604.9 7.8 %copy-start.15 = (bf16[128,2,64]{2,0,1:T(8,128)(2,1)S(1)}, bf16[128,2,64]{2,0,1:T(8,128)(2,1)}, u32[]{:S(2)}) copy-start(bf16[128,2,64]{2,0,1:T(8,128)(2,1)} %copy-done.14) | copy-start | bytes 98308
  604.9 7.9 %copy-start.17 = (bf16[128,256]{1,0:T(8,128)(2,1)S(1)}, bf16[128,256]{1,0:T(8,128)(2,1)}, u32[]{:S(2)}) copy-start(bf16[128,256]{1,0:T(8,128)(2,1)} %copy-done.16) | copy-start | bytes 196612
  604.9 112.6 %all-to-all-start.1 = ((bf16[128,12,2048]{2,1,0:T(8,128)(2,1)}), bf16[128,12,2048]{2,1,0:T(8,128)(2,1)}, u32[]{:S(2)}, u32[]{:S(2)}) async-start(bf16[128,12,2048]{2,1,0:T(8,128)(2,1)} %reshape.352), calls=%async_computation.1 | async-start | bytes 16777216 | tf_op jit(solution)/shard_map/all_to_all | solution.py:201
  (6 other events, 4.7 us)
Sparse Core Ops, SparseCore 0:
  11.1 117.4 all-gather.5
  130.2 45.2 all-gather.11
  179.3 69.6 all-gather.7
  251.6 71.0 all-gather.9
  325.6 103.2 all-gather.13
where the time goes:
time: 762 us; the launch traced here: 756 us
  waiting for transfers between devices  382 us (50%)
  blocking collectives  105 us (14%)
  local copies, waits for them, and re-layouts  102 us (13%)
  matrix products  93.2 us (12%)
  other arithmetic  51.6 us (7%)
  between operations  14.5 us (2%)
  starting transfers between devices  7.85 us (1%)
    all_gather x1, waiting for transfers between devices, local(): lax.all_gather(query_key_value_weight, 'expert', axis=0, tiled=True)  114 us
    all_to_all x1, blocking collectives, local(): lax.all_to_all(outgoing.reshape(expert_count, capacity, width), ('dp', 'e...  105 us
    all_to_all x1, waiting for transfers between devices, local(): lax.all_to_all(results, ('dp', 'expert'), split_axis=0, concat_axis=0, ti...  104 us
    all_gather x1, waiting for transfers between devices, local(): lax.all_gather(w_out, 'expert', axis=0, tiled=True)  73.6 us
    all_gather x1, waiting for transfers between devices, local(): piece_keys = lax.all_gather(key_rows, 'expert', axis=0, tiled=True)  38.8 us
    dot_general x2, matrix products, attend(): jnp.einsum('kgqs,skd->kgqd', weights.astype(jnp.bfloat16), value_rows, pr...  32.7 us
    all_gather x1, waiting for transfers between devices, local(): piece_values = lax.all_gather(value_rows, 'expert', axis=0, tiled=True)  28.9 us
    dot_general x2, matrix products, attend(): jnp.einsum('qkgd,skd->kgqs', queries, key_rows, preferred_element_type=jn...  28.6 us
  transfers between devices with their start and end apart: 6, of which 6 were waited for; matrix products, arithmetic and copies ran while one was open for 18% of the time, Pallas kernels for 0%

commit v1 on v0

--- a/solution.py
+++ b/solution.py
@@ -102,7 +102,12 @@
     part = normed
     qkv = jnp.dot(
         part,
-        lax.all_gather(query_key_value_weight, "expert", axis=0, tiled=True),
+        jnp.concatenate(
+            lax.all_to_all(
+                jnp.stack([query_key_value_weight] * lax.axis_size("expert")), "expert", 0, 0
+            ),
+            axis=0,
+        ),
         preferred_element_type=jnp.float32,
     )
     index = col * tokens_here + jnp.arange(tokens_here, dtype=jnp.int32)

time: 762 us -> 810 us (1.063)
  waiting for transfers between devices: 382 us -> 415 us
  starting transfers between devices: 7.85 us -> 16.7 us
    all_to_all x0 -> x1, waiting for transfers between devices: none -> 178 us  [local(): lax.all_to_all(jnp.stack([query_key_value_weight] * lax.axis_size('expert...]
    all_gather x1 -> x0, waiting for transfers between devices: 114 us -> none  [local(): lax.all_gather(query_key_value_weight, 'expert', axis=0, tiled=True)]
    all_gather x1, waiting for transfers between devices: 21.2 us -> 0.01 us  [local(): piece = lax.all_gather(kv_pool, 'dp', axis=0, tiled=True)]
    all_gather x1, waiting for transfers between devices: 38.8 us -> 29.7 us  [local(): piece_keys = lax.all_gather(key_rows, 'expert', axis=0, tiled=True)]
    all_to_all x0 -> x1, starting transfers between devices: none -> 8.93 us  [local(): lax.all_to_all(jnp.stack([query_key_value_weight] * lax.axis_size('expert...]
  transfers between devices with their start and end apart: 6 -> 6, of which waited for: 6 -> 5; matrix products, arithmetic and copies ran while one was open for 18% -> 17% of each run, Pallas kernels for 0% -> 0%
where the time goes in v1:
time: 810 us; the launch traced here: 803 us
  waiting for transfers between devices  415 us (51%)
  local copies, waits for them, and re-layouts  107 us (13%)
  blocking collectives  105 us (13%)
  matrix products  93.2 us (12%)
  other arithmetic  51.6 us (6%)
  starting transfers between devices  16.7 us (2%)
  between operations  14.5 us (2%)
    all_to_all x1, waiting for transfers between devices, local(): lax.all_to_all(jnp.stack([query_key_value_weight] * lax.axis_size('expert...  178 us
    all_to_all x1, blocking collectives, local(): lax.all_to_all(outgoing.reshape(expert_count, capacity, width), ('dp', 'e...  105 us
    all_to_all x1, waiting for transfers between devices, local(): lax.all_to_all(results, ('dp', 'expert'), split_axis=0, concat_axis=0, ti...  104 us
    all_gather x1, waiting for transfers between devices, local(): lax.all_gather(w_out, 'expert', axis=0, tiled=True)  73.6 us
    dot_general x2, matrix products, attend(): jnp.einsum('kgqs,skd->kgqd', weights.astype(jnp.bfloat16), value_rows, pr...  32.7 us
    all_gather x1, waiting for transfers between devices, local(): piece_keys = lax.all_gather(key_rows, 'expert', axis=0, tiled=True)  29.7 us
    all_gather x1, waiting for transfers between devices, local(): piece_values = lax.all_gather(value_rows, 'expert', axis=0, tiled=True)  29 us
    dot_general x2, matrix products, attend(): jnp.einsum('qkgd,skd->kgqs', queries, key_rows, preferred_element_type=jn...  28.7 us
  transfers between devices with their start and end apart: 6, of which 5 were waited for; matrix products, arithmetic and copies ran while one was open for 17% of the time, Pallas kernels for 0%

profile of v1, /device:TPU:67, one launch (start us, length us, event | category | flops | bytes accessed | tf_op | source)
XLA Modules:
  0.0 803.5 jit_solution(7303006617059966330)
XLA Ops:
  7.2 6.1 stack.2
  13.3 8.9 %all-to-all-start = ((bf16[32,64,2560]{2,1,0:T(8,128)(2,1)}), bf16[32,64,2560]{2,1,0:T(8,128)(2,1)}, u32[]{:S(2)}, u32[]{:S(2)}) async-start(bf16[32,64,2560]{2,1,0:T(8,128)(2,1)} %stack.2), calls=%async_computation | async-start | bytes 20971520 | tf_op jit(solution)/shard_map/all_to_all | solution.py:106
  27.6 178.4 %all-to-all-done = bf16[32,64,2560]{2,1,0:T(8,128)(2,1)} async-done(((bf16[32,64,2560]{2,1,0:T(8,128)(2,1)}), bf16[32,64,2560]{2,1,0:T(8,128)(2,1)}, u32[]{:S(2)}, u32[]{:S(2)}) %all-to-all-start) | async-done | bytes 10485792 | tf_op jit(solution)/shard_map/all_to_all | solution.py:106
  252.7 13.7 %bitcast_reduce_fusion = (f32[2,8,128]{2,1,0:T(8,128)S(1)}, f32[2,128,8,4096]{3,1,2,0:T(8,128)}) fusion(pred[128,4096]{1,0:T(8,128)(4,1)S(1)} %copy-done.2, bf16[4096,2,128,1]{2,0,3,1:T(8,128)(2,1)S(1)} %bitcast.169, bf16[128,2,8,64]{3,0,2,1:T(8,128)(2,1)S(1)} %bitcast.172, bf16[128,2,8,64]{3,0,2,1:T(8,128)(2,1)S(1)} %bitcast.170), kind=kOutput, calls=%fused_computation.3 | convolution fusion | flops 2173696000 | bytes 36708352 | tf_op jit(solution)/shard_map/qkgd,skd->kgqs/dot_general | solution.py:48
  266.4 29.7 %all-gather.5.cloned.1.call-done = bf16[4096,2,128]{2,0,1:T(8,128)(2,1)} async-done(((bf16[128,2,128]{2,0,1:T(8,128)(2,1)}), bf16[4096,2,128]{2,0,1:T(8,128)(2,1)}) %all-gather.5.cloned.1.call-update) | async-done | bytes 2097168 | tf_op jit(solution)/shard_map/all_gather | solution.py:150
  296.2 15.0 %fusion.3 = (f32[2,8,128]{2,1,0:T(8,128)S(1)}, f32[2,4096,128,8]{2,1,3,0:T(8,128)}) fusion(pred[128,4096]{0,1:T(8,128)(4,1)} %fusion.29, bf16[128,2,8,64]{3,0,2,1:T(8,128)(2,1)} %bitcast.173, bf16[128,2,8,64]{3,0,2,1:T(8,128)(2,1)} %bitcast.171, bf16[4096,2,128]{2,0,1:T(8,128)(2,1)} %all-gather.5.cloned.1.call-done), kind=kOutput, calls=%fused_computation.10 | convolution fusion | flops 2173696000 | bytes 36708352 | tf_op jit(solution)/shard_map/qkgd,skd->kgqs/dot_general | solution.py:48
  311.1 16.4 %fusion.1 = f32[2,8,128]{2,1,0:T(8,128)S(1)} fusion(f32[2,4096,128,8]{2,1,3,0:T(8,128)} %get-tuple-element.22, f32[2,8,128]{2,1,0:T(8,128)S(1)} %get-tuple-element.16, pred[128,4096]{0,1:T(8,128)(4,1)S(1)} %copy-done.4), kind=kLoop, calls=%fused_computation.8 | loop fusion | flops 33552384 | bytes 34095104 | tf_op jit(solution)/shard_map/reduce_sum | solution.py:54
  331.4 9.5 %fusion.4 = f32[2,8,128]{2,1,0:T(8,128)S(1)} fusion(f32[2,128,8,4096]{3,1,2,0:T(8,128)S(1)} %copy-done.1, f32[2,8,128]{2,1,0:T(8,128)S(1)} %get-tuple-element.15, pred[128,4096]{1,0:T(8,128)(4,1)S(1)} %copy-done.3), kind=kLoop, calls=%fused_computation.11 | loop fusion | flops 33552384 | bytes 34095104 | tf_op jit(solution)/shard_map/reduce_sum | solution.py:54
  341.0 29.0 %all-gather.7.cloned.1.call-done = bf16[4096,2,128]{0,2,1:T(8,128)(2,1)} async-done(((bf16[128,2,128]{0,2,1:T(8,128)(2,1)}), bf16[4096,2,128]{0,2,1:T(8,128)(2,1)}) %all-gather.7.cloned.1.call-update) | async-done | bytes 2097168 | tf_op jit(solution)/shard_map/all_gather | solution.py:151
  370.0 16.3 %fusion.50 = f32[128,2,8,128]{0,3,2,1:T(8,128)} fusion(f32[2,4096,128,8]{2,1,3,0:T(8,128)} %get-tuple-element.22, f32[2,8,128]{2,1,0:T(8,128)S(1)} %get-tuple-element.16, pred[128,4096]{0,1:T(8,128)(4,1)} %fusion.29, bf16[4096,2,128]{0,2,1:T(8,128)(2,1)} %all-gather.7.cloned.1.call-done, f32[128,2,8]{0,2,1:T(8,128)S(1)} %get-tuple-element.5, ...), kind=kOutput, calls=%fused_computation.45 | convolution fusion | flops 2181562368 | bytes 37249024 | tf_op jit(solution)/shard_map/kgqs,skd->kgqd/dot_general | solution.py:55
  386.3 16.3 %fusion.60 = bf16[128,2,8,128]{0,3,2,1:T(8,128)(2,1)} fusion(f32[128,2,8,128]{0,3,2,1:T(8,128)} %fusion.50, bf16[4096,2,128,1]{0,2,1,3:T(8,128)(2,1)} %reshape.380, f32[2,128,8,4096]{3,1,2,0:T(8,128)} %get-tuple-element.20, f32[2,8,128]{2,1,0:T(8,128)S(1)} %get-tuple-element.15, pred[128,4096]{1,0:T(8,128)(4,1)} %broadcast_compare_fusion, ...), kind=kOutput, calls=%fused_computation.47 | convolution fusion | flops 2181824512 | bytes 37765120 | tf_op jit(solution)/shard_map/kgqs,skd->kgqd/dot_general | solution.py:55
  402.7 73.6 %all-gather.11.cloned.1.call-done = bf16[2048,2048]{1,0:T(8,128)(2,1)} async-done(((bf16[64,2048]{1,0:T(8,128)(2,1)}), bf16[2048,2048]{1,0:T(8,128)(2,1)}) %all-gather.11.cloned.1.call-update) | async-done | bytes 8388624 | tf_op jit(solution)/shard_map/all_gather | solution.py:182
  483.2 10.9 %scatter_custom_fusion = bf16[1536,2048]{1,0:T(8,128)(2,1)} fusion(s32[1024]{0:T(1024)S(1)} %bitcast.177, bf16[]{:T(256)} %constant.80.clone.1, bf16[128,2048]{1,0:T(8,128)(2,1)} %multiply_convert_fusion), kind=kCustom, calls=%fused_computation.24 | custom fusion | bytes 6815746 | tf_op jit(solution)/shard_map/scatter | solution.py:195
  494.1 10.6 %reshape.356 = bf16[128,12,2048]{2,1,0:T(8,128)(2,1)} reshape(bf16[1536,2048]{1,0:T(8,128)(2,1)} %scatter_custom_fusion) | data formatting | bytes 12582912 | tf_op jit(solution)/shard_map/reshape | solution.py:199
  504.7 105.0 %all_to_all.15 = bf16[128,12,2048]{2,1,0:T(8,128)(2,1)} all-to-all(bf16[128,12,2048]{2,1,0:T(8,128)(2,1)} %reshape.356), channel_id=1, replica_groups=mesh['dp'=4,'expert'=32] {'dp','expert'}, dimensions={0} | all-to-all | bytes 12582912 | tf_op jit(solution)/shard_map/all_to_all | solution.py:198
  609.7 10.7 %reshape.357 = bf16[1536,2048]{1,0:T(8,128)(2,1)} reshape(bf16[128,12,2048]{2,1,0:T(8,128)(2,1)} %all_to_all.15) | data formatting | bytes 12582912 | tf_op jit(solution)/shard_map/reshape | solution.py:205
  620.4 14.1 %fusion.13 = f32[1536,1536]{1,0:T(8,128)S(1)} fusion(bf16[1536,2048]{1,0:T(8,128)(2,1)} %reshape.357, bf16[1,2048,1536]{2,1,0:T(8,128)(2,1)} %param.22), kind=kOutput, calls=%fused_computation.20 | convolution fusion | flops 9663676416 | bytes 22020096 | tf_op jit(solution)/shard_map/dot_general | solution.py:65
  634.6 7.1 convolution_convert_fusion
  641.6 10.6 %reshape.358 = bf16[128,12,2048]{2,1,0:T(8,128)(2,1)} reshape(bf16[1536,2048]{1,0:T(8,128)(2,1)} %convolution_convert_fusion) | data formatting | bytes 12582912 | tf_op jit(solution)/shard_map/reshape | solution.py:205
  652.2 7.6 all-to-all-start.2
  660.8 104.1 %all-to-all-done.2 = bf16[128,12,2048]{2,1,0:T(8,128)(2,1)} async-done(((bf16[128,12,2048]{2,1,0:T(8,128)(2,1)}), bf16[128,12,2048]{2,1,0:T(8,128)(2,1)}, u32[]{:S(2)}, u32[]{:S(2)}) %all-to-all-start.2) | async-done | bytes 6291488 | tf_op jit(solution)/shard_map/all_to_all | solution.py:206
  764.8 10.7 %reshape.359 = bf16[1536,2048]{1,0:T(8,128)(2,1)} reshape(bf16[128,12,2048]{2,1,0:T(8,128)(2,1)} %all-to-all-done.2) | data formatting | bytes 12582912 | tf_op jit(solution)/shard_map/reshape | solution.py:207
  775.5 12.4 %gather_fusion = bf16[1024,2048]{1,0:T(8,128)(2,1)} fusion(bf16[1536,2048]{1,0:T(8,128)(2,1)} %reshape.359, s32[1024]{0:T(1024)S(1)} %broadcast_clamp_fusion), kind=kCustom, calls=%fused_computation | custom fusion | bytes 8392704 | tf_op jit(solution)/shard_map/gather | solution.py:207
  788.0 6.5 fusion.12
  (129 shorter events, 65.6 us)
Async XLA Ops:
  7.2 627.4 %copy-start = (bf16[1,768,2048]{2,1,0:T(8,128)(2,1)S(1)}, bf16[1,768,2048]{2,1,0:T(8,128)(2,1)}, u32[]{:S(2)}) copy-start(bf16[1,768,2048]{2,1,0:T(8,128)(2,1)} %param.23) | copy-start | bytes 9437188
  13.3 11.6 %copy-start.24 = (s32[4,4]{1,0:T(4,128)S(1)}, s32[4,4]{1,0:T(4,128)}, u32[]{:S(2)}) copy-start(s32[4,4]{1,0:T(4,128)} %param.26) | copy-start | bytes 196
  13.3 192.6 %copy-start.18 = (f32[2048]{0:T(1024)S(1)}, f32[2048]{0:T(1024)}, u32[]{:S(2)}) copy-start(f32[2048]{0:T(1024)} %param.16) | copy-start | bytes 24580
  13.3 192.6 %all-to-all-start = ((bf16[32,64,2560]{2,1,0:T(8,128)(2,1)}), bf16[32,64,2560]{2,1,0:T(8,128)(2,1)}, u32[]{:S(2)}, u32[]{:S(2)}) async-start(bf16[32,64,2560]{2,1,0:T(8,128)(2,1)} %stack.2), calls=%async_computation | async-start | bytes 20971520 | tf_op jit(solution)/shard_map/all_to_all | solution.py:106
  22.3 209.4 %all-gather.9.cloned.1.call-start = ((), (), s32[]{:S(2)}) async-start(), calls=%async_computation.5 | async-start | bytes 5242880 | tf_op jit(solution)/shard_map/all_gather | solution.py:158
  24.9 271.3 %all-gather.5.cloned.1.call-start = ((), (), s32[]{:S(2)}) async-start(), calls=%async_computation.3 | async-start | bytes 2162688 | tf_op jit(solution)/shard_map/all_gather | solution.py:150
  205.9 10.4 %copy-start.22 = (f32[128]{0:T(128)S(1)}, f32[128]{0:T(128)}, u32[]{:S(2)}) copy-start(f32[128]{0:T(128)} %param.19) | copy-start | bytes 1540
  206.0 14.4 %copy-start.19 = (s32[128,8]{0,1:T(8,128)S(1)}, s32[128,8]{0,1:T(8,128)}, u32[]{:S(2)}) copy-start(s32[128,8]{0,1:T(8,128)} %param.28) | copy-start | bytes 12292
  206.0 17.7 %copy-start.25 = (s32[32]{0:T(128)S(1)}, s32[32]{0:T(128)}, u32[]{:S(2)}) copy-start(s32[32]{0:T(128)} %param.25) | copy-start | bytes 388
  218.0 152.0 %all-gather.7.cloned.1.call-start = ((), (), s32[]{:S(2)}) async-start(), calls=%async_computation.4 | async-start | bytes 2162688 | tf_op jit(solution)/shard_map/all_gather | solution.py:151
  218.9 1.3 copy-start.16
  219.7 256.6 %all-gather.11.cloned.1.call-start = ((), (), s32[]{:S(2)}) async-start(), calls=%async_computation.6 | async-start | bytes 8650752 | tf_op jit(solution)/shard_map/all_gather | solution.py:182
  235.8 13.5 %copy-start.23 = (f32[128]{0:T(128)S(1)}, f32[128]{0:T(128)}, u32[]{:S(2)}) copy-start(f32[128]{0:T(128)} %param.18) | copy-start | bytes 1540
  249.3 3.4 copy-start.2
  249.3 3.4 copy-start.7
  296.2 15.0 %copy-start.4 = (pred[128,4096]{0,1:T(8,128)(4,1)S(1)}, pred[128,4096]{0,1:T(8,128)(4,1)}, u32[]{:S(2)}) copy-start(pred[128,4096]{0,1:T(8,128)(4,1)} %fusion.29) | copy-start | bytes 1572868
  311.1 20.3 %copy-start.1 = (f32[2,128,8,4096]{3,1,2,0:T(8,128)S(1)}, f32[2,128,8,4096]{3,1,2,0:T(8,128)}, u32[]{:S(2)}) copy-start(f32[2,128,8,4096]{3,1,2,0:T(8,128)} %get-tuple-element.20) | copy-start | bytes 100663296
  311.1 20.3 %copy-start.3 = (pred[128,4096]{1,0:T(8,128)(4,1)S(1)}, pred[128,4096]{1,0:T(8,128)(4,1)}, u32[]{:S(2)}) copy-start(pred[128,4096]{1,0:T(8,128)(4,1)} %broadcast_compare_fusion) | copy-start | bytes 1572868
  476.3 6.0 copy-start.20
  652.2 7.7 copy-start.21
  652.2 7.8 copy-start.13
  652.2 7.8 copy-start.15
  652.2 7.9 copy-start.17
  652.2 112.6 %all-to-all-start.2 = ((bf16[128,12,2048]{2,1,0:T(8,128)(2,1)}), bf16[128,12,2048]{2,1,0:T(8,128)(2,1)}, u32[]{:S(2)}, u32[]{:S(2)}) async-start(bf16[128,12,2048]{2,1,0:T(8,128)(2,1)} %reshape.358), calls=%async_computation.2 | async-start | bytes 16777216 | tf_op jit(solution)/shard_map/all_to_all | solution.py:206
  (8 other events, 6.8 us)
Sparse Core Ops, SparseCore 0:
  25.0 83.8 all-gather.8
  218.1 78.0 all-gather.4
  298.9 71.0 all-gather.6
  372.9 103.2 all-gather.10
